TPU v7x, 256 devices: a whole 4x4x8 slice. The times are simulated.
256 devices in a mesh: col: 32 (over z, x), bin: 8 (over y, core).
Axes of the slice: x: 4, y: 4, z: 8, core: 2. Of those that a mesh axis runs over, the one named last changes fastest.
Arguments:
- slope: float32 [262144], P('bin'), may hold values from -6 to 6
- curvature: float32 [262144], P('bin'), may hold values from -6 to 0
- target_mean: float32 [262144], P('bin'), may hold values from 0.15 to 0.85
- target_var: float32 [262144], P('bin'), may hold values from 0.06 to 0.12
- table: float32 [64, 512], P(None, 'col'), may hold values from -6 to 6
Outputs:
- species_mean: float32 [64, 262144], P('col')
- final_slope: float32 [262144], replicated
All inputs are finite; a program needn't handle non-finite values.
Results may differ from a plain program's by a relative error of at most 0.0001.
Values sent between devices are 32-bit elements; how exact they have to be, the bound alone decides.
No kernel may reach another device: no remote copies, remote signals or barrier semaphores. Data moves between devices by JAX's collectives and lax.ppermute only.
A program may use at most 64 MiB of HBM per device.

v0:
```python
import jax
import jax.numpy as jnp
from jax import lax
from jax.sharding import PartitionSpec as P

ITERS = 3


def in_order(blocks, dim):
    blocks = jnp.moveaxis(blocks, 0, dim)
    shape = blocks.shape
    return blocks.reshape(*shape[:dim], shape[dim] * shape[dim + 1], *shape[dim + 2 :])


def copy_for_each(array, axis):
    copies = jnp.broadcast_to(array, (lax.axis_size(axis), *array.shape))
    return lax.all_to_all(copies, axis, split_axis=0, concat_axis=0, tiled=True)


def gather_directly(array, axis, dim):
    return in_order(copy_for_each(array, axis), dim)


def exponent(lam, curvature, points):
    return jnp.exp(lam[None, :] * points + curvature[None, :] * points * points)


def per_device(slope, curvature, target_mean, target_var, table):
    columns = lax.axis_size("col")
    width = slope.shape[0] // columns
    offset = lax.axis_index("col") * width
    own_slope = lax.dynamic_slice_in_dim(slope, offset, width, 0)
    own_curve = lax.dynamic_slice_in_dim(curvature, offset, width, 0)
    own_mean = lax.dynamic_slice_in_dim(target_mean, offset, width, 0)
    own_var = lax.dynamic_slice_in_dim(target_var, offset, width, 0)
    full_table = gather_directly(table, "col", 1)
    total_pts = full_table.shape[1]
    points = ((lax.iota(jnp.int32, total_pts).astype(jnp.float32) + 0.5) / total_pts)[:, None]
    own_lam = own_slope
    for step in range(ITERS):
        expo = exponent(own_lam, own_curve, points)
        partition = jnp.sum(expo, axis=0)
        moment = jnp.sum(points * expo, axis=0)
        own_lam = own_lam + (own_mean - moment / partition) / own_var
    expo = exponent(own_lam, own_curve, points)
    weights = expo / jnp.sum(expo, axis=0)[None, :]
    terms = jnp.dot(
        full_table, weights, precision=lax.Precision.HIGHEST, preferred_element_type=jnp.float32
    )
    species = lax.all_to_all(terms, "col", split_axis=0, concat_axis=1, tiled=True)
    lam = gather_directly(own_lam, "col", 0)
    species_mean, final_slope = (
        lax.all_gather(species, "bin", axis=1, tiled=True),
        lax.all_gather(lam, "bin", axis=0, tiled=True),
    )
    return (species_mean, final_slope)


def solution(mesh):
    placed = (P("bin"), P("bin"), P("bin"), P("bin"), P(None, "col"))
    return jax.shard_map(
        per_device, mesh=mesh, in_specs=placed, out_specs=(P("col", None), P()), check_vma=False
    )
```

profile of v0, /device:TPU:1, one launch (start us, length us, event | category | flops | bytes accessed | tf_op | source)
XLA Modules:
  0.0 104.1 jit_solution(18431287290563344208)
XLA Ops:
  7.2 0.0 copy-start
  7.2 0.0 all-gather.5.cloned.1.call-start
  7.2 0.7 dynamic_slice.14
  7.9 0.7 dynamic_slice.12
  8.6 0.7 fusion.4
  9.3 0.7 divide_add_fusion.2
  10.1 0.7 fusion
  10.8 0.7 divide_add_fusion.1
  11.5 0.7 fusion.1
  12.2 0.7 divide_add_fusion
  12.9 0.1 broadcast_in_dim.5
  13.0 21.1 %all_to_all.30 = f32[32,1,1024]{2,1,0:T(1,128)} all-to-all(f32[32,1,1024]{2,1,0:T(1,128)S(1)} %broadcast_in_dim.5), channel_id=1, replica_groups=mesh['col'=32,'bin'=8] {'col'}, dimensions={0} | all-to-all | bytes 262144 | tf_op jit(solution)/shard_map/all_to_all | solution.py:17
  34.1 0.0 all-gather.5.cloned.1.call-update
  34.1 0.0 copy-done
  34.2 0.8 reshape.32
  35.0 3.9 %all-to-all-start = ((f32[32,1,1024]{2,1,0:T(1,128)}), f32[32,1,1024]{2,1,0:T(1,128)S(1)}, u32[]{:S(2)}, u32[]{:S(2)}) async-start(f32[32,1,1024]{2,1,0:T(1,128)} %reshape.32), calls=%async_computation | async-start | bytes 262144 | tf_op jit(solution)/shard_map/all_to_all | solution.py:17
  38.9 0.0 all-gather.3.cloned.1.call-start
  38.9 0.6 fusion.3
  39.5 8.8 %all-to-all-done = f32[32,1,1024]{2,1,0:T(1,128)S(1)} async-done(((f32[32,1,1024]{2,1,0:T(1,128)}), f32[32,1,1024]{2,1,0:T(1,128)S(1)}, u32[]{:S(2)}, u32[]{:S(2)}) %all-to-all-start) | async-done | bytes 131104 | tf_op jit(solution)/shard_map/all_to_all | solution.py:17
  48.3 0.5 broadcast.18
  48.8 1.0 reduce
  49.8 0.1 reshape.33
  49.9 2.0 %fusion.7 = f32[64,1024]{1,0:T(8,128)S(1)} fusion(f32[64,512]{0,1:T(8,128)S(1)} %bitcast.15, f32[1024]{0:T(1024)S(1)} %fusion.3, f32[1024]{0:T(1024)S(1)} %divide_add_fusion, f32[1024]{0:T(1024)S(1)} %dynamic_slice.14, f32[512]{0:T(512)S(1)} %add_multiply_fusion), kind=kOutput, calls=%fused_computation.14 | convolution fusion | flops 405274624 | bytes 407552 | tf_op jit(solution)/shard_map/dot_general | solution.py:47
  51.9 0.1 all_to_all.22
  52.0 14.2 %all_to_all.31 = f32[32,2,1024]{2,1,0:T(2,128)} all-to-all(f32[32,2,1024]{2,1,0:T(2,128)S(1)} %all_to_all.22), channel_id=1, replica_groups=mesh['col'=32,'bin'=8] {'col'}, dimensions={0} | all-to-all | bytes 524288 | tf_op jit(solution)/shard_map/all_to_all | solution.py:50
  66.3 0.0 all-gather.3.cloned.1.call-update
  66.3 0.0 all-gather.5.cloned.1.call-done
  66.3 0.0 copy-start.1
  66.3 27.3 %all-gather.3.cloned.1.call-done = f32[2,262144]{1,0:T(2,128)} async-done(((f32[2,32768]{1,0:T(2,128)}), f32[2,262144]{1,0:T(2,128)}) %all-gather.3.cloned.1.call-update) | async-done | bytes 2097168 | tf_op jit(solution)/shard_map/all_gather | solution.py:53
  93.6 2.6 %copy.14 = f32[2,262144]{1,0:T(2,128)} copy(f32[2,262144]{1,0:T(2,128)} %all-gather.3.cloned.1.call-done) | data formatting | bytes 4194304
  96.2 0.0 copy-done.1
  96.2 1.0 copy.15
  (2 shorter events, 0.0 us)
Async XLA Ops:
  7.2 27.0 %copy-start = (f32[64,16]{0,1:T(8,128)S(1)}, f32[64,16]{0,1:T(8,128)}, u32[]{:S(2)}) copy-start(f32[64,16]{0,1:T(8,128)} %param.9) | copy-start | bytes 12292
  7.2 59.1 %all-gather.5.cloned.1.call-start = ((), (), s32[]{:S(2)}) async-start(), calls=%async_computation.4 | async-start | bytes 1179648 | tf_op jit(solution)/shard_map/all_gather | solution.py:54
  35.0 13.3 %all-to-all-start = ((f32[32,1,1024]{2,1,0:T(1,128)}), f32[32,1,1024]{2,1,0:T(1,128)S(1)}, u32[]{:S(2)}, u32[]{:S(2)}) async-start(f32[32,1,1024]{2,1,0:T(1,128)} %reshape.32), calls=%async_computation | async-start | bytes 262144 | tf_op jit(solution)/shard_map/all_to_all | solution.py:17
  38.9 54.7 %all-gather.3.cloned.1.call-start = ((), (), s32[]{:S(2)}) async-start(), calls=%async_computation.3 | async-start | bytes 2359296 | tf_op jit(solution)/shard_map/all_gather | solution.py:53
  66.3 29.9 %copy-start.1 = (f32[262144]{0:T(1024)S(1)}, f32[262144]{0:T(1024)}, u32[]{:S(2)}) copy-start(f32[262144]{0:T(1024)} %all-gather.5.cloned.1.call-done) | copy-start | bytes 3145732
Sparse Core Ops, SparseCore 0:
  34.3 22.9 all-gather.4
  66.4 27.1 all-gather.2
where the time goes:
time: 105 us; the launch traced here: 104 us
  waiting for transfers between devices  36.1 us (34%)
  blocking collectives  35.4 us (34%)
  between operations  14.1 us (13%)
  local copies, waits for them, and re-layouts  6.73 us (6%)
  other arithmetic  5.81 us (6%)
  starting transfers between devices  3.94 us (4%)
  matrix products  2.01 us (2%)
    all_gather x1, waiting for transfers between devices, per_device(): lax.all_gather(species, 'bin', axis=1, tiled=True)  27.3 us
    all_to_all x1, blocking collectives, copy_for_each(): return lax.all_to_all(copies, axis, split_axis=0, concat_axis=0, tiled=True)  21.1 us
    all_to_all x1, blocking collectives, per_device(): lax.all_to_all(terms, 'col', split_axis=0, concat_axis=1, tiled=True)  14.2 us
    all_to_all x1, waiting for transfers between devices, copy_for_each(): return lax.all_to_all(copies, axis, split_axis=0, concat_axis=0, tiled=True)  8.78 us
    unnamed x9, local copies, waits for them, and re-layouts  4.62 us
    all_to_all x1, starting transfers between devices, copy_for_each(): return lax.all_to_all(copies, axis, split_axis=0, concat_axis=0, tiled=True)  3.86 us
    add x3, other arithmetic, per_device(): own_lam = own_lam + (own_mean - moment / partition) / own_var  2.17 us
    reduce_sum x3, other arithmetic, per_device(): partition = jnp.sum(expo, axis=0)  2.11 us
  transfers between devices with their start and end apart: 3, of which 2 were waited for; matrix products, arithmetic and copies ran while one was open for 5% of the time, Pallas kernels for 0%

commit v1 on v0

--- a/solution.py
+++ b/solution.py
@@ -50,7 +50,9 @@
     species = lax.all_to_all(terms, "col", split_axis=0, concat_axis=1, tiled=True)
     lam = gather_directly(own_lam, "col", 0)
     species_mean, final_slope = (
-        lax.all_gather(species, "bin", axis=1, tiled=True),
+        jnp.concatenate(
+            lax.all_to_all(jnp.stack([species] * lax.axis_size("bin")), "bin", 0, 0), axis=1
+        ),
         lax.all_gather(lam, "bin", axis=0, tiled=True),
     )
     return (species_mean, final_slope)

time: 105 us -> 111 us (1.057)
  blocking collectives: 35.4 us -> 0 us
  starting transfers between devices: 3.94 us -> 30.6 us
  waiting for transfers between devices: 36.1 us -> 47.7 us
  local copies, waits for them, and re-layouts: 6.73 us -> 9.98 us
    all_to_all x2 -> x0, blocking collectives: 35.4 us -> none  [the longest x1 21.1 us: copy_for_each(): return lax.all_to_all(copies, axis, split_axis=0, concat_axis=0, tiled=True)]
    all_gather x1 -> x0, waiting for transfers between devices: 27.3 us -> none  [per_device(): lax.all_gather(species, 'bin', axis=1, tiled=True)]
    all_to_all x0 -> x2, waiting for transfers between devices: none -> 24.7 us  [the longest x1 15 us: per_device(): lax.all_to_all(jnp.stack([species] * lax.axis_size('bin')), 'bin', 0, 0)]
    all_gather x1, waiting for transfers between devices: 0.02 us -> 14.3 us  [per_device(): lax.all_gather(lam, 'bin', axis=0, tiled=True)]
    all_to_all x1 -> x2, starting transfers between devices: 3.86 us -> 18 us  [copy_for_each(): return lax.all_to_all(copies, axis, split_axis=0, concat_axis=0, tiled=True)]
    all_to_all x0 -> x2, starting transfers between devices: none -> 12.5 us  [the longest x1 8.22 us: per_device(): lax.all_to_all(jnp.stack([species] * lax.axis_size('bin')), 'bin', 0, 0)]
    another operation x0 -> x1, local copies, waits for them, and re-layouts: none -> 1.86 us  [per_device(): jnp.stack([species] * lax.axis_size('bin'))]
    all_to_all x1 -> x2, waiting for transfers between devices: 8.78 us -> 7.98 us  [copy_for_each(): return lax.all_to_all(copies, axis, split_axis=0, concat_axis=0, tiled=True)]
  transfers between devices with their start and end apart: 3 -> 5, of which waited for: 2 -> 5; matrix products, arithmetic and copies ran while one was open for 5% -> 11% of each run, Pallas kernels for 0% -> 0%
where the time goes in v1:
time: 111 us; the launch traced here: 110 us
  waiting for transfers between devices  47.7 us (43%)
  starting transfers between devices  30.6 us (28%)
  between operations  14.1 us (13%)
  local copies, waits for them, and re-layouts  9.98 us (9%)
  other arithmetic  5.82 us (5%)
  matrix products  2.01 us (2%)
    all_to_all x2, starting transfers between devices, copy_for_each(): return lax.all_to_all(copies, axis, split_axis=0, concat_axis=0, tiled=True)  18 us
    all_to_all x1, waiting for transfers between devices, per_device(): lax.all_to_all(jnp.stack([species] * lax.axis_size('bin')), 'bin', 0, 0)  15 us
    all_gather x1, waiting for transfers between devices, per_device(): lax.all_gather(lam, 'bin', axis=0, tiled=True)  14.3 us
    all_to_all x1, waiting for transfers between devices, per_device(): lax.all_to_all(terms, 'col', split_axis=0, concat_axis=1, tiled=True)  9.67 us
    all_to_all x1, starting transfers between devices, per_device(): lax.all_to_all(jnp.stack([species] * lax.axis_size('bin')), 'bin', 0, 0)  8.22 us
    all_to_all x2, waiting for transfers between devices, copy_for_each(): return lax.all_to_all(copies, axis, split_axis=0, concat_axis=0, tiled=True)  7.98 us
    unnamed x11, local copies, waits for them, and re-layouts  4.65 us
    all_to_all x1, starting transfers between devices, per_device(): lax.all_to_all(terms, 'col', split_axis=0, concat_axis=1, tiled=True)  4.3 us
  transfers between devices with their start and end apart: 5, of which 5 were waited for; matrix products, arithmetic and copies ran while one was open for 11% of the time, Pallas kernels for 0%

profile of v1, /device:TPU:1, one launch (start us, length us, event | category | flops | bytes accessed | tf_op | source)
XLA Modules:
  0.0 110.2 jit_solution(5544628281906039682)
XLA Ops:
  7.2 0.0 copy-start
  7.2 0.7 copy-done
  7.9 0.8 reshape.43
  8.7 11.9 %all-to-all-start = ((f32[32,1,1024]{2,1,0:T(1,128)}), f32[32,1,1024]{2,1,0:T(1,128)S(1)}, u32[]{:S(2)}, u32[]{:S(2)}) async-start(f32[32,1,1024]{2,1,0:T(1,128)} %reshape.43), calls=%async_computation | async-start | bytes 262144 | tf_op jit(solution)/shard_map/all_to_all | solution.py:17
  20.6 0.7 dynamic_slice.14
  21.3 0.7 dynamic_slice.12
  22.0 0.7 fusion.4
  22.7 0.7 divide_add_fusion.2
  23.4 0.7 fusion
  24.2 0.7 divide_add_fusion.1
  24.9 0.7 fusion.1
  25.6 0.7 divide_add_fusion
  26.3 0.6 fusion.3
  26.9 3.1 %all-to-all-done = f32[32,1,1024]{2,1,0:T(1,128)S(1)} async-done(((f32[32,1,1024]{2,1,0:T(1,128)}), f32[32,1,1024]{2,1,0:T(1,128)S(1)}, u32[]{:S(2)}, u32[]{:S(2)}) %all-to-all-start) | async-done | bytes 131104 | tf_op jit(solution)/shard_map/all_to_all | solution.py:17
  29.9 0.7 broadcast_in_dim.5
  30.7 6.2 %all-to-all-start.3 = ((f32[32,1,1024]{2,1,0:T(1,128)}), f32[32,1,1024]{2,1,0:T(1,128)S(1)}, u32[]{:S(2)}, u32[]{:S(2)}) async-start(f32[32,1,1024]{2,1,0:T(1,128)} %broadcast_in_dim.5), calls=%async_computation.3 | async-start | bytes 262144 | tf_op jit(solution)/shard_map/all_to_all | solution.py:17
  36.8 0.5 broadcast.19
  37.4 1.0 reduce
  38.3 0.1 reshape.44
  38.4 2.0 %fusion.7 = f32[64,1024]{1,0:T(8,128)S(1)} fusion(f32[64,512]{0,1:T(8,128)S(1)} %bitcast.19, f32[1024]{0:T(1024)S(1)} %fusion.3, f32[1024]{0:T(1024)S(1)} %divide_add_fusion, f32[1024]{0:T(1024)S(1)} %dynamic_slice.14, f32[512]{0:T(512)S(1)} %add_multiply_fusion), kind=kOutput, calls=%fused_computation.14 | convolution fusion | flops 405274624 | bytes 407552 | tf_op jit(solution)/shard_map/dot_general | solution.py:47
  40.4 0.9 all_to_all.23
  41.3 4.9 %all-to-all-done.3 = f32[32,1,1024]{2,1,0:T(1,128)S(1)} async-done(((f32[32,1,1024]{2,1,0:T(1,128)}), f32[32,1,1024]{2,1,0:T(1,128)S(1)}, u32[]{:S(2)}, u32[]{:S(2)}) %all-to-all-start.3) | async-done | bytes 131104 | tf_op jit(solution)/shard_map/all_to_all | solution.py:17
  46.2 0.0 copy-start.2
  46.2 4.3 %all-to-all-start.1 = ((f32[32,2,1024]{2,1,0:T(2,128)}), f32[32,2,1024]{2,1,0:T(2,128)S(1)}, u32[]{:S(2)}, u32[]{:S(2)}) async-start(f32[32,2,1024]{2,1,0:T(2,128)} %all_to_all.23), calls=%async_computation.1 | async-start | bytes 524288 | tf_op jit(solution)/shard_map/all_to_all | solution.py:50
  50.5 0.0 all-gather.2.cloned.1.call-start
  50.5 0.0 copy-done.2
  50.6 0.7 all-gather.2.cloned.1.call-update
  51.2 9.7 %all-to-all-done.1 = f32[32,2,1024]{2,1,0:T(2,128)S(1)} async-done(((f32[32,2,1024]{2,1,0:T(2,128)}), f32[32,2,1024]{2,1,0:T(2,128)S(1)}, u32[]{:S(2)}, u32[]{:S(2)}) %all-to-all-start.1) | async-done | bytes 262176 | tf_op jit(solution)/shard_map/all_to_all | solution.py:50
  60.9 1.9 %stack.5 = f32[8,2,32768]{2,1,0:T(2,128)} broadcast(f32[2,32768]{1,0:T(2,128)S(1)} %bitcast.17), dimensions={1,2} | broadcast | bytes 2359296 | tf_op jit(solution)/shard_map/stack | solution.py:54
  62.8 8.2 %all-to-all-start.2 = ((f32[8,2,32768]{2,1,0:T(2,128)}), f32[8,2,32768]{2,1,0:T(2,128)S(1)}, u32[]{:S(2)}, u32[]{:S(2)}) async-start(f32[8,2,32768]{2,1,0:T(2,128)} %stack.5), calls=%async_computation.2 | async-start | bytes 4194304 | tf_op jit(solution)/shard_map/all_to_all | solution.py:54
  71.0 14.3 %all-gather.2.cloned.1.call-done = f32[262144]{0:T(1024)} async-done(((f32[32768]{0:T(1024)}), f32[262144]{0:T(1024)}) %all-gather.2.cloned.1.call-update) | async-done | bytes 1048592 | tf_op jit(solution)/shard_map/all_gather | solution.py:56
  85.3 15.0 %all-to-all-done.2 = f32[8,2,32768]{2,1,0:T(2,128)S(1)} async-done(((f32[8,2,32768]{2,1,0:T(2,128)}), f32[8,2,32768]{2,1,0:T(2,128)S(1)}, u32[]{:S(2)}, u32[]{:S(2)}) %all-to-all-start.2) | async-done | bytes 2097184 | tf_op jit(solution)/shard_map/all_to_all | solution.py:54
  100.3 0.0 copy-start.1
  100.3 1.3 %copy.10 = f32[2,262144]{1,0:T(2,128)} copy(f32[2,262144]{1,0:T(2,128)S(1)} %bitcast.16) | data formatting | bytes 4194304
  101.7 0.6 copy-done.1
  102.3 1.0 copy.11
  (2 shorter events, 0.0 us)
Async XLA Ops:
  7.2 0.7 copy-start
  8.7 21.2 %all-to-all-start = ((f32[32,1,1024]{2,1,0:T(1,128)}), f32[32,1,1024]{2,1,0:T(1,128)S(1)}, u32[]{:S(2)}, u32[]{:S(2)}) async-start(f32[32,1,1024]{2,1,0:T(1,128)} %reshape.43), calls=%async_computation | async-start | bytes 262144 | tf_op jit(solution)/shard_map/all_to_all | solution.py:17
  30.7 15.5 %all-to-all-start.3 = ((f32[32,1,1024]{2,1,0:T(1,128)}), f32[32,1,1024]{2,1,0:T(1,128)S(1)}, u32[]{:S(2)}, u32[]{:S(2)}) async-start(f32[32,1,1024]{2,1,0:T(1,128)} %broadcast_in_dim.5), calls=%async_computation.3 | async-start | bytes 262144 | tf_op jit(solution)/shard_map/all_to_all | solution.py:17
  46.2 4.4 %copy-start.2 = (f32[32,1,1024]{2,1,0:T(1,128)}, f32[32,1,1024]{2,1,0:T(1,128)S(1)}, u32[]{:S(2)}) copy-start(f32[32,1,1024]{2,1,0:T(1,128)S(1)} %all-to-all-done.3) | copy-start | bytes 393220
  46.2 14.7 %all-to-all-start.1 = ((f32[32,2,1024]{2,1,0:T(2,128)}), f32[32,2,1024]{2,1,0:T(2,128)S(1)}, u32[]{:S(2)}, u32[]{:S(2)}) async-start(f32[32,2,1024]{2,1,0:T(2,128)} %all_to_all.23), calls=%async_computation.1 | async-start | bytes 524288 | tf_op jit(solution)/shard_map/all_to_all | solution.py:50
  50.5 34.8 %all-gather.2.cloned.1.call-start = ((), (), s32[]{:S(2)}) async-start(), calls=%async_computation.4 | async-start | bytes 1179648 | tf_op jit(solution)/shard_map/all_gather | solution.py:56
  62.8 37.6 %all-to-all-start.2 = ((f32[8,2,32768]{2,1,0:T(2,128)}), f32[8,2,32768]{2,1,0:T(2,128)S(1)}, u32[]{:S(2)}, u32[]{:S(2)}) async-start(f32[8,2,32768]{2,1,0:T(2,128)} %stack.5), calls=%async_computation.2 | async-start | bytes 4194304 | tf_op jit(solution)/shard_map/all_to_all | solution.py:54
  100.3 2.0 %copy-start.1 = (f32[262144]{0:T(1024)S(1)}, f32[262144]{0:T(1024)}, u32[]{:S(2)}) copy-start(f32[262144]{0:T(1024)} %all-gather.2.cloned.1.call-done) | copy-start | bytes 3145732
Sparse Core Ops, SparseCore 0:
  53.2 32.0 all-gather.1
